TPU v7x, 768 devices: a whole 4x8x12 slice. The times are simulated.
768 devices in a mesh: row: 12 (over z_lo, x), col: 64 (over y, z_hi, core).
Axes of the slice: x: 4, y: 8, z: 12 (z_hi: 4, z_lo: 3; z = z_hi * 3 + z_lo), core: 2. Of those that a mesh axis runs over, the one named last changes fastest.
Arguments:
- grad_out: bfloat16 [98304, 128], P(('row', 'col')), may hold values from -6 to 6
- pre_act: bfloat16 [98304, 128], P(('row', 'col')), may hold values from -6 to 6
- features: bfloat16 [98304, 128], P(('row', 'col')), may hold values from -6 to 6
- weight: bfloat16 [128, 128], replicated, may hold values from -0.5 to 0.5
- blocks: bfloat16 [12, 64, 64, 2, 128, 128], P('row', 'col'), may hold values from -0.046875 to 0.046875
- block_cols: int32 [12, 64, 64, 2], P('row', 'col'), may hold values from 0 to 11
- block_counts: int32 [12, 64, 64], P('row', 'col'), may hold values from 0 to 2, as said below
- order: int32 [98304], P(('row', 'col')), may hold values from 0 to 127, as said below
Outputs:
- grad_feat: bfloat16 [98304, 128], P(('row', 'col'))
- weight_grad: float32 [128, 128], replicated
Inputs may be any that keep to these rules, and one draw needn't show every extreme that they name: `block_counts`: every device's slice has at least one row block with 2 nonzero blocks. `order`: each slab of 128 entries is a permutation of 0 to 127.
All inputs are finite; a program needn't handle non-finite values.
Results may differ from a plain program's by a relative error of at most 0.019.
Values may be sent and summed in bfloat16 or wider, within the bound.
A program may use at most 64 MiB of HBM per device.

v0:
```python
import jax
import jax.numpy as jnp
from jax import lax
from jax.sharding import PartitionSpec as P

F = 128
B = 128
K = 2


def shards(grad_out, pre_act, features, weight, blocks, block_cols, block_counts, order):
    slab_rows = grad_out.shape[0]
    row_count = lax.axis_size("row")
    col_count = lax.axis_size("col")
    targets = row_count * (slab_rows // B)
    masked = jnp.where(pre_act > 0, grad_out, jnp.zeros_like(grad_out))
    masked_block = jnp.take(masked, order, axis=0)
    feat_block = jnp.take(features, order, axis=0)
    block_vals = blocks[0, 0]
    columns = block_cols[0, 0]
    counts = block_counts[0, 0]
    filled = jnp.arange(K, dtype=jnp.int32)[None, :] < counts[:, None]
    hits = columns[:, :, None] == jnp.arange(targets, dtype=jnp.int32)[None, None, :]
    selector = jnp.where(hits & filled[:, :, None], 1.0, 0.0).astype(jnp.float32)
    region = lax.all_gather(masked_block, "col", axis=0, tiled=True)
    count_rows = region.shape[0]
    blk_count = count_rows // B
    panel_rows = region.reshape(blk_count, B, F)
    products = jnp.einsum(
        "ikrc,irf->ikcf", block_vals, panel_rows, preferred_element_type=jnp.float32
    )
    partial_value = jnp.einsum("ikj,ikcf->jcf", selector, products, precision=lax.Precision.HIGHEST)
    owned_sum = lax.psum_scatter(
        partial_value.reshape(targets * B, F).astype(jnp.bfloat16),
        "row",
        scatter_dimension=0,
        tiled=True,
    )
    grad_block = lax.dot_general(
        owned_sum, weight, (((1,), (1,)), ((), ())), preferred_element_type=jnp.float32
    ).astype(jnp.bfloat16)
    grad_feat = jnp.zeros_like(grad_block).at[order].set(grad_block)
    partial_w = lax.dot_general(
        feat_block, owned_sum, (((0,), (0,)), ((), ())), preferred_element_type=jnp.float32
    )
    summed_w = lax.psum(partial_w, ("row", "col"))
    node_total = slab_rows * row_count * col_count
    return (grad_feat, summed_w * node_total ** (-0.5))


def solution(mesh):
    placed = (
        P(("row", "col"), None),
        P(("row", "col"), None),
        P(("row", "col"), None),
        P(),
        P("row", "col", None, None, None, None),
        P("row", "col", None, None),
        P("row", "col", None),
        P(("row", "col")),
    )
    return jax.shard_map(
        shards,
        mesh=mesh,
        in_specs=placed,
        out_specs=(P(("row", "col"), None), P()),
        check_vma=False,
    )
```

profile of v0, /device:TPU:1, one launch (start us, length us, event | category | flops | bytes accessed | tf_op | source)
XLA Modules:
  0.0 671.4 jit_solution(593656973524660739)
XLA Ops:
  7.2 0.0 copy-start
  7.2 0.0 all-gather.2.cloned.1.call-start
  7.2 0.7 compare_select_fusion.1
  7.9 0.7 compare_and_fusion
  8.6 0.8 compare_select_fusion
  9.3 0.7 gather_fusion
  10.0 0.7 broadcast_select_fusion
  10.7 0.0 all-gather.2.cloned.1.call-update
  10.8 0.0 reduce-scatter.2.cloned.1.call-start
  10.8 0.7 iota_compare_fusion.1
  11.5 103.4 %all-gather.2.cloned.1.call-done = bf16[8192,128]{1,0:T(8,128)(2,1)} async-done(((bf16[128,128]{1,0:T(8,128)(2,1)}), bf16[8192,128]{1,0:T(8,128)(2,1)}) %all-gather.2.cloned.1.call-update) | async-done | bytes 2097168 | tf_op jit(solution)/shard_map/all_gather | solution.py:25
  114.9 7.3 %fusion.2 = f32[64,128,2,128]{3,1,2,0:T(8,128)} fusion(bf16[64,128,128,1]{2,1,3,0:T(8,128)(2,1)} %bitcast.30, bf16[1,1,64,2,128,128]{5,4,3,2,1,0:T(8,128)(2,1)} %param.14), kind=kOutput, calls=%fused_computation.5 | convolution fusion | flops 536870912 | bytes 14680064 | tf_op jit(solution)/shard_map/ikrc,irf->ikcf/dot_general | solution.py:29
  122.2 0.0 copy-start.2
  122.2 8.8 %copy.12 = f32[64,128,2,128]{1,0,2,3:T(8,128)} copy(f32[64,128,2,128]{3,1,2,0:T(8,128)} %fusion.2) | data formatting | bytes 16777216 | tf_op jit(solution)/shard_map/ikrc,irf->ikcf/dot_general | solution.py:29
  131.0 0.0 copy-done.2
  131.0 0.0 copy-start.1
  131.0 6.4 fusion.7
  137.4 0.8 copy.10
  138.2 0.0 reduce-scatter.2.cloned.1.call-update
  138.3 0.0 all-reduce.2.cloned.1.call-start
  138.3 0.0 copy-done
  138.3 0.7 gather_fusion.1
  139.0 51.9 %reduce-scatter.2.cloned.1.call-done = bf16[128,128]{1,0:T(8,128)(2,1)} async-done(((bf16[1536,128]{1,0:T(8,128)(2,1)}), bf16[128,128]{1,0:T(8,128)(2,1)}) %reduce-scatter.2.cloned.1.call-update) | async-done | bytes 32784 | tf_op jit(solution)/shard_map/reduce_scatter | solution.py:33
  190.9 1.6 fusion.10
  192.6 0.0 all-reduce.2.cloned.1.call-update
  192.6 0.0 copy-done.1
  192.6 0.9 convolution_convert_fusion
  193.5 1.5 scatter_custom_fusion
  195.0 468.4 %all-reduce.2.cloned.1.call-done = f32[128,128]{1,0:T(8,128)} async-done(((f32[128,128]{1,0:T(8,128)}), f32[128,128]{1,0:T(8,128)}) %all-reduce.2.cloned.1.call-update) | async-done | bytes 65552 | tf_op jit(solution)/shard_map/psum | solution.py:46
  663.4 1.5 broadcast_multiply_fusion
  (1 shorter events, 0.0 us)
Async XLA Ops:
  7.2 131.1 %copy-start = (bf16[128,128]{1,0:T(8,128)(2,1)S(1)}, bf16[128,128]{1,0:T(8,128)(2,1)}, u32[]{:S(2)}) copy-start(bf16[128,128]{1,0:T(8,128)(2,1)} %param.12) | copy-start | bytes 98308
  7.2 107.7 %all-gather.2.cloned.1.call-start = ((), (), s32[]{:S(2)}) async-start(), calls=%async_computation.1 | async-start | bytes 2129920 | tf_op jit(solution)/shard_map/all_gather | solution.py:25
  10.8 180.2 %reduce-scatter.2.cloned.1.call-start = ((), (), s32[]{:S(2)}) async-start(), calls=%async_computation.2 | async-start | bytes 425984 | tf_op jit(solution)/shard_map/reduce_scatter | solution.py:33
  122.2 8.8 %copy-start.2 = (s32[1,1,64,2]{2,3,1,0:T(2,128)S(1)}, s32[1,1,64,2]{2,3,1,0:T(2,128)}, u32[]{:S(2)}) copy-start(s32[1,1,64,2]{2,3,1,0:T(2,128)} %param.15) | copy-start | bytes 1540
  131.0 61.6 %copy-start.1 = (bf16[128,128]{1,0:T(8,128)(2,1)S(1)}, bf16[128,128]{1,0:T(8,128)(2,1)}, u32[]{:S(2)}) copy-start(bf16[128,128]{1,0:T(8,128)(2,1)} %param.13) | copy-start | bytes 98308
  138.3 525.1 %all-reduce.2.cloned.1.call-start = ((), (), s32[]{:S(2)}) async-start(), calls=%async_computation.3 | async-start | bytes 131072 | tf_op jit(solution)/shard_map/psum | solution.py:46
Sparse Core Ops, SparseCore 0:
  12.4 102.3 all-gather.1
  138.4 52.5 reduce-scatter.1
  196.9 466.4 all-reduce.1
where the time goes:
time: 674 us; the launch traced here: 671 us
  waiting for transfers between devices  624 us (93%)
  matrix products  16.2 us (2%)
  between operations  13.8 us (2%)
  local copies, waits for them, and re-layouts  12.5 us (2%)
    psum x1, waiting for transfers between devices, shards(): summed_w = lax.psum(partial_w, ('row', 'col'))  468 us
    all_gather x1, waiting for transfers between devices, shards(): region = lax.all_gather(masked_block, 'col', axis=0, tiled=True)  103 us
    reduce_scatter x1, waiting for transfers between devices, shards(): lax.psum_scatter(partial_value.reshape(targets * B, F).astype(jnp.bfloat1...  51.9 us
  transfers between devices with their start and end apart: 3, of which 3 were waited for; matrix products, arithmetic and copies ran while one was open for 1% of the time, Pallas kernels for 0%

commit v1 on v0

v1 whole, which is shorter than its diff:
```python
import functools

import jax
import jax.numpy as jnp
from jax import lax
from jax.experimental import pallas as pl
from jax.experimental.pallas import tpu as pltpu
from jax.sharding import PartitionSpec as P

F = 128
B = 128
K = 2
NX = 4
NZL = 3
NY = 8
NZH = 4
NCORE = 2
ROWS = NZL * NX
COLS = NY * NZH * NCORE
MESH = pl.DeviceIdType.MESH


def col_of(y, zh, core):
    return (y * NZH + zh) * NCORE + core


def row_of(zl, x):
    return zl * NX + x


def place():
    row = lax.axis_index("row")
    col = lax.axis_index("col")
    zl = row // NX
    x = row % NX
    y = col // (NZH * NCORE)
    zh = (col // NCORE) % NZH
    core = col % NCORE
    return row, col, zl, x, y, zh, core


def remote(src, dst, ssem, rsem, row, col):
    return pltpu.make_async_remote_copy(
        src_ref=src,
        dst_ref=dst,
        send_sem=ssem,
        recv_sem=rsem,
        device_id=(row, col),
        device_id_type=MESH,
    )


def far(q):
    return q + q // 2 - 2 * (q // 3)


def one_hot(order_row):
    nodes = lax.broadcasted_iota(jnp.int32, (B, B), 0)
    return jnp.where(nodes == order_row, 1.0, 0.0).astype(jnp.bfloat16)


def gather_kernel(grad_ref, pre_ref, order_ref, reg, zs, zr, rs, rr, ls, lr, ps, pr):
    row, col, zl, x, y, zh, core = place()
    right = (y + 1) % NY
    left = (y + NY - 1) % NY
    partner = col_of(y, zh, 1 - core)

    barrier = pltpu.get_barrier_semaphore()
    peers = [col_of(right, zh, core), col_of(left, zh, core), partner]
    peers += [col_of(y, (zh + d) % NZH, core) for d in range(1, NZH)]
    for peer in peers:
        pl.semaphore_signal(barrier, inc=1, device_id=(row, peer), device_id_type=MESH)

    masked = jnp.where(pre_ref[...] > 0, grad_ref[...], jnp.zeros_like(grad_ref))
    own = lax.dot_general(
        masked,
        one_hot(order_ref[...]),
        (((0,), (0,)), ((), ())),
        preferred_element_type=jnp.float32,
    )
    reg[pl.ds(col, 1)] = own.astype(jnp.bfloat16)[None]
    pl.semaphore_wait(barrier, len(peers))

    def z_copy(d):
        return remote(
            reg.at[col], reg.at[col], zs.at[d - 1], zr.at[d - 1], row, col_of(y, (zh + d) % NZH, core)
        )

    for d in (1, 3, 2):
        z_copy(d).start()

    def slot(s, q):
        return col_of((y + NY + s) % NY, (zh + NZH - far(q)) % NZH, core)

    def view(index, s, forward):
        if s < NY // 2:
            return reg.at[index]
        return reg.at[index, pl.ds(0 if forward else B // 2, B // 2)]

    def r_copy(s, q):
        ref = view(slot(1 - s, q), s, True)
        return remote(ref, ref, rs.at[s - 1, q], rr.at[s - 1, q], row, col_of(right, zh, core))

    def l_copy(s, q):
        ref = view(slot(s - 1, q), s, False)
        return remote(ref, ref, ls.at[s - 1, q], lr.at[s - 1, q], row, col_of(left, zh, core))

    def got_r(s, q):
        ref = view(slot(-s, q), s, True)
        remote(ref, ref, rs.at[s - 1, q], rr.at[s - 1, q], row, col_of(right, zh, core)).wait_recv()

    def got_l(s, q):
        ref = view(slot(s, q), s, False)
        remote(ref, ref, ls.at[s - 1, q], lr.at[s - 1, q], row, col_of(left, zh, core)).wait_recv()

    def share(s, q):
        index = slot(s, q)
        remote(reg.at[index], reg.at[index], ps, pr, row, partner).start()

    for q in range(NZH):
        if q:
            d = (0, 1, 3, 2)[q]
            src = reg.at[slot(0, q)]
            remote(src, src, zs.at[d - 1], zr.at[d - 1], row, partner).wait_recv()
        r_copy(1, q).start()
        l_copy(1, q).start()
        share(0, q)

    half = NY // 2
    for s in range(1, half):

        def step(q, carry, s=s):
            got_r(s, q)
            r_copy(s + 1, q).start()
            share(-s, q)
            got_l(s, q)
            l_copy(s + 1, q).start()
            share(s, q)
            return carry

        lax.fori_loop(0, NZH, step, 0)

    def last(q, carry):
        got_r(half, q)
        got_l(half, q)
        share(half, q)
        return carry

    lax.fori_loop(0, NZH, last, 0)

    shared = reg.at[pl.ds(0, COLS // 2)]
    remote(shared, shared, ps, pr, row, partner).wait()
    for d in range(1, NZH):
        z_copy(d).wait_send()
    for s in range(1, half + 1):

        def sent(q, carry, s=s):
            r_copy(s, q).wait_send()
            l_copy(s, q).wait_send()
            return carry

        lax.fori_loop(0, NZH, sent, 0)


def gathered(grad_out, pre_act, order):
    return pl.pallas_call(
        gather_kernel,
        out_shape=jax.ShapeDtypeStruct((COLS, F, B), jnp.bfloat16),
        in_specs=[pl.BlockSpec(memory_space=pltpu.VMEM)] * 3,
        out_specs=pl.BlockSpec(memory_space=pltpu.VMEM),
        scratch_shapes=[
            pltpu.SemaphoreType.DMA((NZH - 1,)),
            pltpu.SemaphoreType.DMA((NZH - 1,)),
            pltpu.SemaphoreType.DMA((NY // 2, NZH)),
            pltpu.SemaphoreType.DMA((NY // 2, NZH)),
            pltpu.SemaphoreType.DMA((NY // 2, NZH)),
            pltpu.SemaphoreType.DMA((NY // 2, NZH)),
            pltpu.SemaphoreType.DMA,
            pltpu.SemaphoreType.DMA,
        ],
        compiler_params=pltpu.CompilerParams(collective_id=0, has_side_effects=True),
        name="gather",
    )(grad_out, pre_act, order)


TILE = 8


def product_kernel(target_ref, region_ref, blocks_ref, out_ref, acc, prod):
    step = pl.program_id(0)

    @pl.when(step == 0)
    def _():
        acc[...] = jnp.zeros_like(acc)

    for i in range(TILE):
        panel = region_ref[i]
        for k in range(K):
            prod[i * K + k] = jnp.dot(panel, blocks_ref[i, k], preferred_element_type=jnp.float32)
    for n in range(TILE * K):
        j = target_ref[step * (TILE * K) + n]
        acc[j] += prod[n]

    @pl.when(step == pl.num_programs(0) - 1)
    def _():
        out_ref[...] = acc[pl.ds(0, ROWS)].astype(jnp.bfloat16)


def partials(target, region, block_vals):
    count = block_vals.shape[0]
    return pl.pallas_call(
        product_kernel,
        out_shape=jax.ShapeDtypeStruct((ROWS, F, B), jnp.bfloat16),
        grid_spec=pltpu.PrefetchScalarGridSpec(
            num_scalar_prefetch=1,
            grid=(count // TILE,),
            in_specs=[
                pl.BlockSpec((TILE, F, B), lambda i, t: (i, 0, 0)),
                pl.BlockSpec((TILE, K, B, B), lambda i, t: (i, 0, 0, 0)),
            ],
            out_specs=pl.BlockSpec((ROWS, F, B), lambda i, t: (0, 0, 0)),
            scratch_shapes=[
                pltpu.VMEM((ROWS + 1, F, B), jnp.float32),
                pltpu.VMEM((TILE * K, F, B), jnp.float32),
            ],
        ),
        name="products",
    )(target, region, block_vals)


CHUNKS = NY * NCORE
CH = F // CHUNKS


def reduce_kernel(
    scale,
    part_ref,
    feat_ref,
    weight_ref,
    order_ref,
    grad_ref,
    wout_ref,
    rbuf,
    wsend,
    b1,
    b2,
    b3,
    b4,
    ssem,
    rsem,
):
    row, col, zl, x, y, zh, core = place()
    mine = y * NCORE + core
    z = zh * NZL + zl
    nz = NZL * NZH

    def row_peer(d):
        return (row + d) % ROWS, col

    def chunk_peer(d):
        q = (mine + d) % CHUNKS
        return row, col_of(q // NCORE, zh, q % NCORE)

    def z_peer(d):
        zz = (z + d) % nz
        return row_of(zz % NZL, x), col_of(y, zz // NZL, core)

    def x_peer(d):
        return row_of(zl, (x + d) % NX), col

    barrier = pltpu.get_barrier_semaphore()
    total = 0
    for peer, n in ((row_peer, ROWS), (chunk_peer, CHUNKS), (z_peer, nz), (x_peer, NX)):

        def greet(d, carry, peer=peer):
            pl.semaphore_signal(barrier, inc=1, device_id=peer(d), device_id_type=MESH)
            return carry

        lax.fori_loop(1, n, greet, 0)
        total += n - 1
    pl.semaphore_wait(barrier, total)

    def send_all(phase, n, src, dst, peer):
        def send(d, carry):
            r, c = peer(d)
            remote(src(d), dst(d), ssem.at[phase], rsem.at[phase], r, c).start()
            return carry

        lax.fori_loop(1, n, send, 0)

    def wait_all(phase, n, buf):
        ref = buf.at[pl.ds(0, n - 1)]
        remote(ref, ref, ssem.at[phase], rsem.at[phase], row, col).wait_recv()

    def wait_sent(phase, n, buf):
        ref = buf.at[pl.ds(0, n - 1)]
        remote(ref, ref, ssem.at[phase], rsem.at[phase], row, col).wait_send()

    send_all(0, ROWS, lambda d: part_ref.at[(row + d) % ROWS], lambda d: rbuf.at[d - 1], row_peer)
    total_sum = part_ref[row].astype(jnp.float32)
    wait_all(0, ROWS, rbuf)
    for d in range(ROWS - 1):
        total_sum += rbuf[d].astype(jnp.float32)
    owned_t = total_sum.astype(jnp.bfloat16)
    nodes = lax.dot_general(
        one_hot(order_ref[...]), owned_t, (((1,), (1,)), ((), ())), preferred_element_type=jnp.float32
    ).astype(jnp.bfloat16)
    partial_w = lax.dot_general(
        feat_ref[...], nodes, (((0,), (0,)), ((), ())), preferred_element_type=jnp.float32
    )
    wsend[...] = partial_w.reshape(CHUNKS, CH, F)

    def chunk_of(d):
        return (mine + d) % CHUNKS

    send_all(1, CHUNKS, lambda d: wsend.at[chunk_of(d)], lambda d: b1.at[d - 1], chunk_peer)
    grad_ref[...] = lax.dot_general(
        nodes, weight_ref[...], (((1,), (1,)), ((), ())), preferred_element_type=jnp.float32
    ).astype(jnp.bfloat16)
    wait_all(1, CHUNKS, b1)
    value = wsend[mine]
    for d in range(CHUNKS - 1):
        value += b1[d]
    b2[pl.ds(z, 1)] = value[None]
    send_all(2, nz, lambda d: b2.at[z], lambda d: b2.at[z], z_peer)
    wait_all(2, nz, b2)
    value = b2[0]
    for d in range(1, nz):
        value += b2[d]
    b3[pl.ds(x, 1)] = value[None]
    send_all(3, NX, lambda d: b3.at[x], lambda d: b3.at[x], x_peer)
    wait_all(3, NX, b3)
    value = b3[0]
    for d in range(1, NX):
        value += b3[d]
    b4[pl.ds(mine, 1)] = (value * scale)[None]
    send_all(4, CHUNKS, lambda d: b4.at[mine], lambda d: b4.at[mine], chunk_peer)
    wait_all(4, CHUNKS, b4)
    wout_ref[...] = b4[...].reshape(F, F)
    wait_sent(0, ROWS, rbuf)
    wait_sent(1, CHUNKS, b1)
    wait_sent(2, nz, b2)
    wait_sent(3, NX, b3)
    wait_sent(4, CHUNKS, b4)


def reduced(scale, part, features, weight, order):
    nz = NZL * NZH
    return pl.pallas_call(
        functools.partial(reduce_kernel, scale),
        out_shape=(
            jax.ShapeDtypeStruct((B, F), jnp.bfloat16),
            jax.ShapeDtypeStruct((F, F), jnp.float32),
        ),
        in_specs=[pl.BlockSpec(memory_space=pltpu.VMEM)] * 4,
        out_specs=(pl.BlockSpec(memory_space=pltpu.VMEM), pl.BlockSpec(memory_space=pltpu.VMEM)),
        scratch_shapes=[
            pltpu.VMEM((ROWS - 1, F, B), jnp.bfloat16),
            pltpu.VMEM((CHUNKS, CH, F), jnp.float32),
            pltpu.VMEM((CHUNKS - 1, CH, F), jnp.float32),
            pltpu.VMEM((nz, CH, F), jnp.float32),
            pltpu.VMEM((NX, CH, F), jnp.float32),
            pltpu.VMEM((CHUNKS, CH, F), jnp.float32),
            pltpu.SemaphoreType.DMA((5,)),
            pltpu.SemaphoreType.DMA((5,)),
        ],
        compiler_params=pltpu.CompilerParams(collective_id=1, has_side_effects=True),
        name="reduce",
    )(part, features, weight, order)


def shards(grad_out, pre_act, features, weight, blocks, block_cols, block_counts, order):
    order_row = order.reshape(1, B)
    region = gathered(grad_out, pre_act, order_row)
    filled = jnp.arange(K, dtype=jnp.int32)[None, :] < block_counts[0, 0][:, None]
    target = jnp.where(filled, block_cols[0, 0], ROWS).reshape(-1)
    part = partials(target, region, blocks[0, 0])
    scale = float(B * ROWS * COLS) ** -0.5
    return reduced(scale, part, features, weight, order_row)


def solution(mesh):
    placed = (
        P(("row", "col"), None),
        P(("row", "col"), None),
        P(("row", "col"), None),
        P(),
        P("row", "col", None, None, None, None),
        P("row", "col", None, None),
        P("row", "col", None),
        P(("row", "col")),
    )
    return jax.shard_map(
        shards,
        mesh=mesh,
        in_specs=placed,
        out_specs=(P(("row", "col"), None), P()),
        check_vma=False,
    )
```

time: 674 us -> 94 us (0.14)
  waiting for transfers between devices: 624 us -> 0 us
  Pallas kernels: 0 us -> 87.7 us
  matrix products: 16.2 us -> 0 us
  between operations: 13.8 us -> 0.66 us
  local copies, waits for them, and re-layouts: 12.5 us -> 3.9 us
    psum x1 -> x0, waiting for transfers between devices: 468 us -> none  [shards(): summed_w = lax.psum(partial_w, ('row', 'col'))]
    all_gather x1 -> x0, waiting for transfers between devices: 103 us -> none  [shards(): region = lax.all_gather(masked_block, 'col', axis=0, tiled=True)]
    pallas_call x0 -> x3, Pallas kernels: none -> 87.7 us  [the longest x1 40.6 us: gathered(): pl.pallas_call(gather_kernel, out_shape=jax.ShapeDtypeStruct((COLS, F, B)...]
    reduce_scatter x1 -> x0, waiting for transfers between devices: 51.9 us -> none  [shards(): lax.psum_scatter(partial_value.reshape(targets * B, F).astype(jnp.bfloat1...]
    dot_general x4 -> x0, matrix products: 16.2 us -> none  [the longest x1 7.34 us: shards(): jnp.einsum('ikrc,irf->ikcf', block_vals, panel_rows, preferred_element_ty...]
    dot_general x1 -> x0, local copies, waits for them, and re-layouts: 8.78 us -> none  [shards(): jnp.einsum('ikrc,irf->ikcf', block_vals, panel_rows, preferred_element_ty...]
  transfers between devices with their start and end apart: 3 -> 0, of which waited for: 3 -> 0; matrix products, arithmetic and copies ran while one was open for 1% -> 0% of each run, Pallas kernels for 0% -> 0%
where the time goes in v1:
time: 94 us; the launch traced here: 93.5 us
  Pallas kernels  87.7 us (93%)
  local copies, waits for them, and re-layouts  3.9 us (4%)
  other arithmetic  1.25 us (1%)
    pallas_call x1, Pallas kernels, gathered(): pl.pallas_call(gather_kernel, out_shape=jax.ShapeDtypeStruct((COLS, F, B)...  40.6 us
    pallas_call x1, Pallas kernels, reduced(): pl.pallas_call(functools.partial(reduce_kernel, scale), out_shape=(jax.Sh...  39.4 us
    pallas_call x1, Pallas kernels, partials(): pl.pallas_call(product_kernel, out_shape=jax.ShapeDtypeStruct((ROWS, F, B...  7.76 us
    unnamed x3, local copies, waits for them, and re-layouts  3.62 us

profile of v1, /device:TPU:1, one launch (start us, length us, event | category | flops | bytes accessed | tf_op | source)
XLA Modules:
  0.0 93.5 jit_solution(5194739696641213703)
XLA Ops:
  0.6 0.7 iota_compare_fusion
  1.4 0.1 lt.23
  1.5 0.8 copy.11
  2.3 0.1 squeeze.6
  2.4 0.5 broadcast_select_fusion.target_ref
  2.9 40.6 %gather.1.region_ref = bf16[64,128,128]{2,1,0:T(8,128)(2,1)} custom-call(bf16[128,128]{1,0:T(8,128)(2,1)} %grad_ref.1, bf16[128,128]{1,0:T(8,128)(2,1)} %pre_ref.1, s32[1,128]{1,0:T(1,128)} %bitcast.6), custom_call_target="tpu_custom_call" | custom-call | tf_op jit(solution)/shard_map/gather/pallas_call | solution.py:166
  43.5 7.8 %products.1.part_ref = bf16[12,128,128]{2,1,0:T(8,128)(2,1)} custom-call(s32[128]{0:T(128)} %broadcast_select_fusion.target_ref, bf16[64,128,128]{2,1,0:T(8,128)(2,1)} %gather.1.region_ref, bf16[64,2,128,128]{3,2,1,0:T(8,128)(2,1)} %bitcast.5), custom_call_target="tpu_custom_call" | custom-call | tf_op jit(solution)/shard_map/products/pallas_call | solution.py:211
  51.3 39.4 %reduce.1 = (bf16[128,128]{1,0:T(8,128)(2,1)}, f32[128,128]{1,0:T(8,128)}) custom-call(bf16[12,128,128]{2,1,0:T(8,128)(2,1)} %products.1.part_ref, bf16[128,128]{1,0:T(8,128)(2,1)} %feat_ref.1, bf16[128,128]{1,0:T(8,128)(2,1)} %weight_ref.1, s32[1,128]{1,0:T(1,128)} %bitcast.7), custom_call_target="tpu_custom_call" | custom-call | tf_op jit(solution)/shard_map/reduce/pallas_call | solution.py:349
  90.7 1.4 %copy.14 = bf16[128,128]{1,0:T(8,128)(2,1)} copy(bf16[128,128]{1,0:T(8,128)(2,1)} %get-tuple-element.4) | data formatting | bytes 65536
  92.1 1.5 %copy.15 = f32[128,128]{1,0:T(8,128)} copy(f32[128,128]{1,0:T(8,128)} %get-tuple-element.5) | data formatting | bytes 131072

commit v2 on v0

v2 whole, which is shorter than its diff:
```python
import functools

import jax
import jax.numpy as jnp
from jax import lax
from jax.experimental import pallas as pl
from jax.experimental.pallas import tpu as pltpu
from jax.sharding import PartitionSpec as P

F = 128
B = 128
K = 2
NX = 4
NZL = 3
NY = 8
NZH = 4
NCORE = 2
ROWS = NZL * NX
COLS = NY * NZH * NCORE
MESH = pl.DeviceIdType.MESH


def col_of(y, zh, core):
    return (y * NZH + zh) * NCORE + core


def row_of(zl, x):
    return zl * NX + x


def place():
    row = lax.axis_index("row")
    col = lax.axis_index("col")
    zl = row // NX
    x = row % NX
    y = col // (NZH * NCORE)
    zh = (col // NCORE) % NZH
    core = col % NCORE
    return row, col, zl, x, y, zh, core


def remote(src, dst, ssem, rsem, row, col):
    return pltpu.make_async_remote_copy(
        src_ref=src,
        dst_ref=dst,
        send_sem=ssem,
        recv_sem=rsem,
        device_id=(row, col),
        device_id_type=MESH,
    )


def far(q):
    return q + q // 2 - 2 * (q // 3)


def one_hot(order_row):
    nodes = lax.broadcasted_iota(jnp.int32, (B, B), 0)
    return jnp.where(nodes == order_row, 1.0, 0.0).astype(jnp.bfloat16)


CHUNKS = NY * NCORE
CH = F // CHUNKS
NZ = NZL * NZH
HALF = NY // 2
STAGES = tuple((t - o, q) for t in range(1, HALF + 3) for q, o in enumerate((0, 1, 1, 2)) if 1 <= t - o <= HALF)


def kernel(
    scale,
    cols_ref,
    counts_ref,
    grad_ref,
    pre_ref,
    order_ref,
    feat_ref,
    weight_ref,
    blocks_ref,
    gout_ref,
    wout_ref,
    reg,
    blk,
    run,
    prod,
    fbuf,
    part,
    rbuf,
    wsend,
    b1,
    b2,
    b3,
    b4,
    last,
    bsem,
    zs,
    zr,
    rs,
    rr,
    ls,
    lr,
    ps,
    pr,
    ssem,
    rsem,
):
    row, col, zl, x, y, zh, core = place()
    right = (y + 1) % NY
    left = (y + NY - 1) % NY
    partner = col_of(y, zh, 1 - core)
    mine = y * NCORE + core
    z = zh * NZL + zl

    def row_peer(d):
        return (row + d) % ROWS, col

    def chunk_peer(d):
        q = (mine + d) % CHUNKS
        return row, col_of(q // NCORE, zh, q % NCORE)

    def z_peer(d):
        zz = (z + d) % NZ
        return row_of(zz % NZL, x), col_of(y, zz // NZL, core)

    def x_peer(d):
        return row_of(zl, (x + d) % NX), col

    fetch = pltpu.make_async_copy(blocks_ref, blk, bsem)
    fetch.start()

    barrier = pltpu.get_barrier_semaphore()
    total = 0
    for peer, n in ((z_peer, NZ), (chunk_peer, CHUNKS), (row_peer, ROWS), (x_peer, NX)):

        def greet(d, carry, peer=peer):
            pl.semaphore_signal(barrier, inc=1, device_id=peer(d), device_id_type=MESH)
            return carry

        lax.fori_loop(1, n, greet, 0)
        total += n - 1

    masked = jnp.where(pre_ref[...] > 0, grad_ref[...], jnp.zeros_like(grad_ref))
    hot = one_hot(order_ref[...])
    own = lax.dot_general(masked, hot, (((0,), (0,)), ((), ())), preferred_element_type=jnp.float32)
    reg[pl.ds(col, 1)] = own.astype(jnp.bfloat16)[None]
    feat = lax.dot_general(hot, feat_ref[...], (((0,), (0,)), ((), ())), preferred_element_type=jnp.float32)
    fbuf[pl.ds(row, 1)] = feat.astype(jnp.bfloat16)[None]
    run[COLS * K] = jnp.zeros((F, B), jnp.float32)
    for j in range(ROWS):
        last[j] = COLS * K
    pl.semaphore_wait(barrier, total)

    def send_all(phase, n, src, dst, peer):
        def send(d, carry):
            r, c = peer(d)
            remote(src(d), dst(d), ssem.at[phase], rsem.at[phase], r, c).start()
            return carry

        lax.fori_loop(1, n, send, 0)

    def wait_all(phase, n, buf):
        ref = buf.at[pl.ds(0, n - 1)]
        remote(ref, ref, ssem.at[phase], rsem.at[phase], row, partner).wait_recv()

    def wait_sent(phase, n, buf):
        ref = buf.at[pl.ds(0, n - 1)]
        remote(ref, ref, ssem.at[phase], rsem.at[phase], row, partner).wait_send()

    def z_copy(d):
        return remote(
            reg.at[col], reg.at[col], zs.at[d - 1], zr.at[d - 1], row, col_of(y, (zh + d) % NZH, core)
        )

    def slot(s, q, c=None):
        return col_of((y + NY + s) % NY, (zh + NZH - far(q)) % NZH, core if c is None else c)

    def view(index, s, forward):
        if s < HALF:
            return reg.at[index]
        return reg.at[index, pl.ds(0 if forward else F // 2, F // 2)]

    def r_copy(s, q):
        ref = view(slot(1 - s, q), s, True)
        return remote(ref, ref, rs.at[s - 1, q], rr.at[s - 1, q], row, col_of(right, zh, core))

    def l_copy(s, q):
        ref = view(slot(s - 1, q), s, False)
        return remote(ref, ref, ls.at[s - 1, q], lr.at[s - 1, q], row, col_of(left, zh, core))

    def got_r(s, q):
        ref = view(slot(-s, q), s, True)
        remote(ref, ref, rs.at[s - 1, q], rr.at[s - 1, q], row, col_of(right, zh, core)).wait_recv()

    def got_l(s, q):
        ref = view(slot(s, q), s, False)
        remote(ref, ref, ls.at[s - 1, q], lr.at[s - 1, q], row, col_of(left, zh, core)).wait_recv()

    def share(s, q):
        ref = reg.at[slot(s, q)]
        return remote(ref, ref, ps.at[s + HALF - 1, q], pr.at[s + HALF - 1, q], row, partner)

    def got_share(s, q):
        ref = reg.at[slot(s, q, 1 - core)]
        remote(ref, ref, ps.at[s + HALF - 1, q], pr.at[s + HALF - 1, q], row, partner).wait_recv()

    def process(indices):
        for n, i in enumerate(indices):
            panel = reg[i]
            for k in range(K):
                prod[n * K + k] = jnp.dot(panel, blk[i, k], preferred_element_type=jnp.float32)
        for n, i in enumerate(indices):
            for k in range(K):
                j = jnp.where(k < counts_ref[0, i], cols_ref[k, i], ROWS)
                before = [last[t] for t in range(ROWS)]
                prev = jnp.int32(COLS * K)
                for t in range(ROWS):
                    prev = jnp.where(j == t, before[t], prev)
                at = i * K + k
                run[at] = prod[n * K + k] + run[prev]
                for t in range(ROWS):
                    last[t] = jnp.where(j == t, at, before[t])

    def offsets(s):
        return (s,) if s in (0, HALF) else (-s, s)

    def start(q):
        if q:
            d = (0, 1, 3, 2)[q]
            ref = reg.at[slot(0, q)]
            remote(ref, ref, zs.at[d - 1], zr.at[d - 1], row, partner).wait_recv()
        r_copy(1, q).start()
        l_copy(1, q).start()
        share(0, q).start()

    done = []

    def drain(s, q):
        indices = [slot(o, q) for o in offsets(s)]
        if done:
            ps_, pq_ = done[-1]
            for o in offsets(ps_):
                got_share(o, pq_)
                indices.append(slot(o, pq_, 1 - core))
        done.append((s, q))
        process(indices)

    for d in (1, 3, 2):
        z_copy(d).start()
    start(0)
    fetch.wait()
    drain(0, 0)
    for s, q in STAGES:
        got_r(s, q)
        if s < HALF:
            r_copy(s + 1, q).start()
        if s < HALF:
            share(-s, q).start()
        got_l(s, q)
        if s < HALF:
            l_copy(s + 1, q).start()
        share(s, q).start()
        if (s, q) == (1, 0):
            start(1)
            start(2)
            send_all(5, ROWS, lambda d: fbuf.at[row], lambda d: fbuf.at[row], row_peer)
            drain(s, q)
            drain(0, 1)
            drain(0, 2)
        elif (s, q) == (1, 2):
            start(3)
            drain(s, q)
            drain(0, 3)
        else:
            drain(s, q)
    s, q = done[-1]
    rest = []
    for o in offsets(s):
        got_share(o, q)
        rest.append(slot(o, q, 1 - core))
    process(rest)

    for j in range(ROWS):
        part[j] = run[last[j]].astype(jnp.bfloat16)
    send_all(0, ROWS, lambda d: part.at[(row + d) % ROWS], lambda d: rbuf.at[d - 1], row_peer)
    wait_all(5, ROWS, fbuf)
    weight_sum = jnp.zeros((F, F), jnp.float32)
    for j in range(ROWS):
        weight_sum += jnp.dot(part[j], fbuf[j], preferred_element_type=jnp.float32)
    wsend[...] = weight_sum.reshape(CHUNKS, CH, F)
    send_all(1, CHUNKS, lambda d: wsend.at[(mine + d) % CHUNKS], lambda d: b1.at[d - 1], chunk_peer)

    wait_all(1, CHUNKS, b1)
    value = wsend[mine]
    for d in range(CHUNKS - 1):
        value += b1[d]
    b2[pl.ds(z, 1)] = value[None]
    send_all(2, NZ, lambda d: b2.at[z], lambda d: b2.at[z], z_peer)

    wait_all(0, ROWS, rbuf)
    owned = part[row].astype(jnp.float32)
    for d in range(ROWS - 1):
        owned += rbuf[d].astype(jnp.float32)
    nodes = lax.dot_general(
        one_hot(order_ref[...]),
        owned.astype(jnp.bfloat16),
        (((1,), (1,)), ((), ())),
        preferred_element_type=jnp.float32,
    ).astype(jnp.bfloat16)
    gout_ref[...] = lax.dot_general(
        nodes, weight_ref[...], (((1,), (1,)), ((), ())), preferred_element_type=jnp.float32
    ).astype(jnp.bfloat16)

    wait_all(2, NZ, b2)
    value = b2[0]
    for d in range(1, NZ):
        value += b2[d]
    b3[pl.ds(x, 1)] = value[None]
    send_all(3, NX, lambda d: b3.at[x], lambda d: b3.at[x], x_peer)

    for d in range(1, NZH):
        z_copy(d).wait_send()
    for s in range(1, HALF + 1):

        def sent(q, carry, s=s):
            r_copy(s, q).wait_send()
            l_copy(s, q).wait_send()
            return carry

        lax.fori_loop(0, NZH, sent, 0)
    for s in range(1 - HALF, HALF + 1):

        def given(q, carry, s=s):
            share(s, q).wait_send()
            return carry

        lax.fori_loop(0, NZH, given, 0)
    wait_sent(5, ROWS, fbuf)
    wait_sent(0, ROWS, rbuf)
    wait_sent(1, CHUNKS, b1)
    wait_sent(2, NZ, b2)

    wait_all(3, NX, b3)
    value = b3[0]
    for d in range(1, NX):
        value += b3[d]
    b4[pl.ds(mine, 1)] = (value * scale)[None]
    send_all(4, CHUNKS, lambda d: b4.at[mine], lambda d: b4.at[mine], chunk_peer)
    wait_all(4, CHUNKS, b4)
    wout_ref[...] = b4[...].reshape(F, F)
    wait_sent(3, NX, b3)
    wait_sent(4, CHUNKS, b4)


def whole(scale, cols, counts, grad_out, pre_act, order, features, weight, block_vals):
    vmem = pl.BlockSpec(memory_space=pltpu.VMEM)
    smem = pl.BlockSpec(memory_space=pltpu.SMEM)
    dma = pltpu.SemaphoreType.DMA
    return pl.pallas_call(
        functools.partial(kernel, scale),
        out_shape=(
            jax.ShapeDtypeStruct((B, F), jnp.bfloat16),
            jax.ShapeDtypeStruct((F, F), jnp.float32),
        ),
        in_specs=[smem, smem, vmem, vmem, vmem, vmem, vmem, pl.BlockSpec(memory_space=pl.ANY)],
        out_specs=(vmem, vmem),
        scratch_shapes=[
            pltpu.VMEM((COLS, F, B), jnp.bfloat16),
            pltpu.VMEM((COLS, K, B, B), jnp.bfloat16),
            pltpu.VMEM((COLS * K + 1, F, B), jnp.float32),
            pltpu.VMEM((4 * K, F, B), jnp.float32),
            pltpu.VMEM((ROWS, B, F), jnp.bfloat16),
            pltpu.VMEM((ROWS, F, B), jnp.bfloat16),
            pltpu.VMEM((ROWS - 1, F, B), jnp.bfloat16),
            pltpu.VMEM((CHUNKS, CH, F), jnp.float32),
            pltpu.VMEM((CHUNKS - 1, CH, F), jnp.float32),
            pltpu.VMEM((NZ, CH, F), jnp.float32),
            pltpu.VMEM((NX, CH, F), jnp.float32),
            pltpu.VMEM((CHUNKS, CH, F), jnp.float32),
            pltpu.SMEM((ROWS,), jnp.int32),
            dma,
            dma((NZH - 1,)),
            dma((NZH - 1,)),
            dma((HALF, NZH)),
            dma((HALF, NZH)),
            dma((HALF, NZH)),
            dma((HALF, NZH)),
            dma((NY, NZH)),
            dma((NY, NZH)),
            dma((6,)),
            dma((6,)),
        ],
        compiler_params=pltpu.CompilerParams(
            collective_id=0, has_side_effects=True, vmem_limit_bytes=40 * 1024 * 1024
        ),
        name="whole",
    )(cols, counts, grad_out, pre_act, order, features, weight, block_vals)


def shards(grad_out, pre_act, features, weight, blocks, block_cols, block_counts, order):
    scale = float(B * ROWS * COLS) ** -0.5
    grad_feat, weight_t = whole(
        scale,
        block_cols[0, 0].T,
        block_counts[0],
        grad_out,
        pre_act,
        order.reshape(1, B),
        features,
        weight,
        blocks[0, 0],
    )
    return grad_feat, weight_t.T


def solution(mesh):
    placed = (
        P(("row", "col"), None),
        P(("row", "col"), None),
        P(("row", "col"), None),
        P(),
        P("row", "col", None, None, None, None),
        P("row", "col", None, None),
        P("row", "col", None),
        P(("row", "col")),
    )
    return jax.shard_map(
        shards,
        mesh=mesh,
        in_specs=placed,
        out_specs=(P(("row", "col"), None), P()),
        check_vma=False,
    )
```

time: 674 us -> 77.6 us (0.12)
  waiting for transfers between devices: 624 us -> 0 us
  Pallas kernels: 0 us -> 67.9 us
  matrix products: 16.2 us -> 0 us
  between operations: 13.8 us -> 0.66 us
    psum x1 -> x0, waiting for transfers between devices: 468 us -> none  [shards(): summed_w = lax.psum(partial_w, ('row', 'col'))]
    all_gather x1 -> x0, waiting for transfers between devices: 103 us -> none  [shards(): region = lax.all_gather(masked_block, 'col', axis=0, tiled=True)]
    pallas_call x0 -> x1, Pallas kernels: none -> 67.9 us  [whole(): pl.pallas_call(functools.partial(kernel, scale), out_shape=(jax.ShapeDtyp...]
    reduce_scatter x1 -> x0, waiting for transfers between devices: 51.9 us -> none  [shards(): lax.psum_scatter(partial_value.reshape(targets * B, F).astype(jnp.bfloat1...]
    dot_general x4 -> x0, matrix products: 16.2 us -> none  [the longest x1 7.34 us: shards(): jnp.einsum('ikrc,irf->ikcf', block_vals, panel_rows, preferred_element_ty...]
    dot_general x1 -> x0, local copies, waits for them, and re-layouts: 8.78 us -> none  [shards(): jnp.einsum('ikrc,irf->ikcf', block_vals, panel_rows, preferred_element_ty...]
    unnamed x6 -> x18, local copies, waits for them, and re-layouts: 0.02 us -> 8.54 us
  transfers between devices with their start and end apart: 3 -> 0, of which waited for: 3 -> 0; matrix products, arithmetic and copies ran while one was open for 1% -> 0% of each run, Pallas kernels for 0% -> 0%
where the time goes in v2:
time: 77.6 us; the launch traced here: 77.1 us
  Pallas kernels  67.9 us (88%)
  local copies, waits for them, and re-layouts  8.54 us (11%)
    pallas_call x1, Pallas kernels, whole(): pl.pallas_call(functools.partial(kernel, scale), out_shape=(jax.ShapeDtyp...  67.9 us
    unnamed x18, local copies, waits for them, and re-layouts  8.54 us

profile of v2, /device:TPU:1, one launch (start us, length us, event | category | flops | bytes accessed | tf_op | source)
XLA Modules:
  0.0 77.1 jit_solution(7687545476715953557)
XLA Ops:
  0.6 0.0 copy-start
  0.6 2.2 %copy-done = bf16[1,1,64,2,128,128]{5,4,3,2,1,0:T(8,128)(2,1)S(1)} copy-done((bf16[1,1,64,2,128,128]{5,4,3,2,1,0:T(8,128)(2,1)S(1)}, bf16[1,1,64,2,128,128]{5,4,3,2,1,0:T(8,128)(2,1)}, u32[]{:S(2)}) %copy-start) | copy-done | bytes 4194328
  2.8 0.0 copy-start.1
  2.8 0.8 copy-done.1
  3.6 0.0 copy-start.2
  3.6 0.8 copy-done.2
  4.3 0.0 copy-start.3
  4.3 0.8 copy-done.3
  5.1 0.0 copy-start.4
  5.1 0.8 copy-done.4
  5.9 0.0 copy-start.5
  5.9 0.7 copy-done.5
  6.5 0.0 copy-start.6
  6.5 0.7 copy-done.6
  7.2 0.0 copy-start.7
  7.2 0.7 copy-done.7
  7.8 67.9 %whole.1 = (bf16[128,128]{1,0:T(8,128)(2,1)S(1)}, f32[128,128]{1,0:T(8,128)S(1)}) custom-call(s32[2,64]{1,0:T(2,128)S(1)} %bitcast.9, s32[1,64]{1,0:T(1,128)S(1)} %bitcast.10, bf16[128,128]{1,0:T(8,128)(2,1)S(1)} %copy-done.1, bf16[128,128]{1,0:T(8,128)(2,1)S(1)} %copy-done.2, s32[1,128]{1,0:T(1,128)S(1)} %bitcast.11, bf16[128,128]{1,0:T(8,128)(2,1)S(1)} %copy-done.3, ...), custom_call_target="tpu_custom_call" | custom-call | tf_op jit(solution)/shard_map/whole/pallas_call | solution.py:357
  75.8 0.7 copy.10
  76.5 0.6 copy.12
Async XLA Ops:
  0.6 2.2 %copy-start = (bf16[1,1,64,2,128,128]{5,4,3,2,1,0:T(8,128)(2,1)S(1)}, bf16[1,1,64,2,128,128]{5,4,3,2,1,0:T(8,128)(2,1)}, u32[]{:S(2)}) copy-start(bf16[1,1,64,2,128,128]{5,4,3,2,1,0:T(8,128)(2,1)} %param.12) | copy-start | bytes 12582916
  2.8 0.8 copy-start.1
  3.6 0.8 copy-start.2
  4.3 0.8 copy-start.3
  5.1 0.8 copy-start.4
  5.9 0.7 copy-start.5
  6.5 0.7 copy-start.6
  7.2 0.7 copy-start.7
